TPU v7x, 256 devices: a whole 4x4x8 slice. The times are simulated.
256 devices in a mesh: row: 8 (over y, x_lo), col: 32 (over z, x_hi, core).
Axes of the slice: x: 4 (x_hi: 2, x_lo: 2; x = x_hi * 2 + x_lo), y: 4, z: 8, core: 2. Of those that a mesh axis runs over, the one named last changes fastest.
Arguments:
- blocks: bfloat16 [32, 4096, 8192], P('row', 'col'), may hold values from -1800 to 1800, as said below
- factor_b: float32 [8192, 256], P('col'), may hold values from -6 to 6
- factor_c: float32 [64, 256], replicated, may hold values from -0.75 to 0.75
- block_pos: int32 [32, 32], P('row', 'col'), may hold values from 0 to 7, as said below
- block_count: int32 [8, 32], P('row', 'col'), may hold values from 1 to 4, as said below
Outputs:
- factor_a_new: float32 [4096, 256], P(('row', 'col'))
- factor_b_new: float32 [8192, 256], P(('col', 'row'))
Inputs may be any that keep to these rules, and one draw needn't show every extreme that they name: `blocks`: every entry is finite. `block_pos`: the 4 positions of one device are distinct. `block_count`: some device has all 4 slots live.
All inputs are finite; a program needn't handle non-finite values.
Results may differ from a plain program's by a relative error of at most 0.007.
Values may be sent and summed in bfloat16 or wider, within the bound.
A program may use at most 64 MiB of HBM per device.

v0:
```python
import jax
import jax.numpy as jnp
from jax import lax
from jax.sharding import PartitionSpec as P

IB_DEV = 4
JB_DEV = 2
norm_eps = 1e-06


def solve_right(rows_in, matrix):
    lower = jnp.linalg.cholesky(matrix)
    half = lax.linalg.triangular_solve(
        lower, rows_in, left_side=False, lower=True, transpose_a=True
    )
    return lax.linalg.triangular_solve(lower, half, left_side=False, lower=True, transpose_a=False)


def body(blocks, factor_b, factor_c, block_pos, block_count):
    high = lax.Precision.HIGHEST
    tile_side = blocks.shape[1]
    depth = factor_c.shape[0]
    rank_width = factor_c.shape[1]
    col_slab = factor_b.shape[0]
    row_slab = IB_DEV * tile_side
    live_count = block_count[0, 0]
    positions = block_pos[:, 0]
    c_low = factor_c.astype(jnp.bfloat16)
    b_low = factor_b.astype(jnp.bfloat16)
    gram_c = jnp.dot(factor_c.T, factor_c, precision=high)
    gram_b = lax.psum(jnp.dot(factor_b.T, factor_b, precision=high), "col")
    v_one = gram_b * gram_c

    def cube_of(index):
        tile = lax.dynamic_index_in_dim(blocks, index, 0, keepdims=False)
        return tile.reshape(tile_side, tile_side, depth)

    def first_term(cube, b_tile):
        inner = lax.dot_general(
            cube, c_low, (((2,), (0,)), ((), ())), preferred_element_type=jnp.float32
        )
        return jnp.sum(inner * b_tile.astype(jnp.float32)[None], axis=1)

    def second_term(cube, a_tile):
        inner = lax.dot_general(
            cube, c_low, (((2,), (0,)), ((), ())), preferred_element_type=jnp.float32
        )
        return jnp.sum(inner * a_tile.astype(jnp.float32)[:, None, :], axis=0)

    def mode_one(index, total):
        place = positions[index]
        b_tile = lax.dynamic_slice_in_dim(b_low, place % JB_DEV * tile_side, tile_side, 0)
        term = first_term(cube_of(index), b_tile)
        start = place // JB_DEV * tile_side
        old = lax.dynamic_slice_in_dim(total, start, tile_side, 0)
        return lax.dynamic_update_slice_in_dim(total, old + term, start, 0)

    partial_a = lax.fori_loop(
        0, live_count, mode_one, jnp.zeros((row_slab, rank_width), jnp.float32)
    )
    rows_total = row_slab * lax.axis_size("row")
    share_rows = row_slab // lax.axis_size("col")
    sum_a = lax.psum(partial_a, "col")
    new_full = solve_right(sum_a, v_one)
    gram_a = lax.psum(jnp.dot(new_full.T, new_full, precision=high), "row")
    scale_a = jnp.sqrt(jnp.diagonal(gram_a) / rows_total + norm_eps)
    hat_full = new_full / scale_a[None, :]
    slab_low = hat_full.astype(jnp.bfloat16)
    hat_a = lax.dynamic_slice_in_dim(hat_full, lax.axis_index("col") * share_rows, share_rows, 0)
    v_two = gram_a / (scale_a[:, None] * scale_a[None, :]) * gram_c

    def mode_two(index, total):
        place = positions[index]
        a_tile = lax.dynamic_slice_in_dim(slab_low, place // JB_DEV * tile_side, tile_side, 0)
        term = second_term(cube_of(index), a_tile)
        start = place % JB_DEV * tile_side
        old = lax.dynamic_slice_in_dim(total, start, tile_side, 0)
        return lax.dynamic_update_slice_in_dim(total, old + term, start, 0)

    partial_b = lax.fori_loop(
        0, live_count, mode_two, jnp.zeros((col_slab, rank_width), jnp.float32)
    )
    part_b = lax.psum_scatter(partial_b, "row", scatter_dimension=0, tiled=True)
    new_b = solve_right(part_b, v_two)
    squares_b = lax.psum(jnp.sum(new_b * new_b, axis=0), ("row", "col"))
    scale_b = jnp.sqrt(squares_b / (col_slab * lax.axis_size("col")) + norm_eps)
    hat_b = new_b / scale_b[None, :]
    return (hat_a, hat_b)


def solution(mesh):
    return jax.shard_map(
        body,
        mesh=mesh,
        in_specs=(P("row", "col", None), P("col", None), P(), P("row", "col"), P("row", "col")),
        out_specs=(P(("row", "col"), None), P(("col", "row"), None)),
        check_vma=False,
    )
```

profile of v0, /device:TPU:1, one launch (start us, length us, event | category | flops | bytes accessed | tf_op | source)
XLA Modules:
  0.0 723.0 jit_solution(14343702082353428203)
XLA Ops:
  7.2 1.0 convert_element_type.22
  8.2 2.3 fusion.33
  10.5 12.0 %copy.17 = bf16[4,128,8192]{1,2,0:T(8,128)(2,1)} copy(bf16[4,128,8192]{2,1,0:T(8,128)(2,1)} %param.10) | data formatting | bytes 16777216 | tf_op jit(solution)/shard_map/while | solution.py:58
  22.5 26.2 %while.26 = (s32[]{:T(128)}, f32[512,256]{1,0:T(8,128)S(1)}, s32[]{:T(128)}, s32[4]{0:T(128)S(1)}, bf16[4,128,8192]{1,2,0:T(8,128)(2,1)}, /*index=5*/bf16[64,256...) while((s32[]{:T(128)}, f32[512,256]{1,0:T(8,128)S(1)}, ...), condition=%wide.region_2.3_spmd, body=%wide.region_0.2_spmd.sunk | while | flops 545292288 | bytes 11370982 | solution.py:58
  23.2 0.6 dynamic_slice.71
  26.1 1.7 constant_dynamic-slice_fusion.11
  27.8 3.5 copy.34
  31.3 4.0 multiply_reduce_fusion.5
  36.0 0.6 dynamic_slice.71
  38.9 1.7 constant_dynamic-slice_fusion.11
  40.6 3.5 copy.34
  44.1 4.0 multiply_reduce_fusion.5
  48.8 0.9 copy-done.1
  49.7 0.4 all-reduce.5.cloned.1.call-start
  50.1 300.5 %all-reduce.7.cloned.1.call-done = (f32[512,256]{1,0:T(8,128)}, f32[256,256]{0,1:T(8,128)}) async-done(((f32[512,256]{1,0:T(8,128)}, f32[256,256]{0,1:T(8,128)}), (f32[512,256]{1,0:T(8,128)}, f32[256,256]{0,1:T(8,128)})) %all-reduce.7.cloned.1.call-update) | async-done | bytes 786448 | tf_op jit(solution)/shard_map/psum | solution.py:63
  350.6 1.4 fusion.32
  352.2 11.7 %cholesky.130 = f32[128,128]{1,0:T(8,128)S(1)} custom-call(f32[128,128]{1,0:T(8,128)S(1)} %cholesky.194), custom_call_target="Cholesky" | custom-call | tf_op jit(solution)/shard_map/jit(cholesky)/cholesky | solution.py:12
  364.0 9.8 %custom-call.23 = f32[1,128,128]{1,2,0:T(8,128)S(1)} custom-call(f32[1,128,128]{2,1,0:T(8,128)S(1)} %get-tuple-element.295), custom_call_target="InvertDiagBlocksLowerTriangular" | custom-call | tf_op jit(solution)/shard_map/jit(cholesky)/cholesky | solution.py:12
  374.0 0.3 convolution_subtract_fusion.3
  374.3 11.7 %cholesky.147 = f32[128,128]{1,0:T(8,128)S(1)} custom-call(f32[128,128]{1,0:T(8,128)S(1)} %convolution_subtract_fusion.3), custom_call_target="Cholesky" | custom-call | tf_op jit(solution)/shard_map/jit(cholesky)/cholesky | solution.py:12
  386.0 0.7 compare_reduce_fusion.2
  388.1 15.6 %while.28 = (s32[]{:T(128)}, f32[256,256]{1,0:T(8,128)S(1)}, s32[2,2]{1,0:T(2,128)S(1)}, f32[2,128,128]{2,1,0:T(8,128)S(1)}, s32[]{:T(128)}) while((s32[]{:T(128)}, f32[256,256]{1,0:T(8,128)S(1)}, s32[2,2]{1,0:T(2,128)S(1)}, f32[2,128,128]{2,1,0:T(8,128)S(1)}, s32[]{:T(128)}) %tuple.97), condition=%wide.while_cond, body=%wide.while_body.sunk | while | flops 2 | bytes 131189 | solution.py:13
  399.8 0.6 fusion.64
  400.4 1.4 bitcast_dynamic-update-slice_fusion.4
  401.8 0.6 fusion.64
  402.4 1.4 bitcast_dynamic-update-slice_fusion.4
  403.7 19.7 %custom-call.18 = f32[2,128,128]{1,2,0:T(8,128)S(1)} custom-call(f32[2,128,128]{2,1,0:T(8,128)S(1)} %get-tuple-element.202), custom_call_target="InvertDiagBlocksLowerTriangular" | custom-call | tf_op jit(solution)/shard_map/triangular_solve | solution.py:13
  423.4 0.4 fusion.4
  423.8 0.4 convolution_subtract_fusion.1
  424.2 0.4 fusion.16
  424.6 0.4 fusion.15
  425.0 0.6 convolution_subtract_fusion
  425.6 0.4 fusion.14
  425.9 1.3 fusion.3
  427.4 73.3 %all-reduce.5.cloned.1.call-done = f32[256,256]{0,1:T(8,128)} async-done(((f32[256,256]{0,1:T(8,128)}), f32[256,256]{0,1:T(8,128)}) %all-reduce.5.cloned.1.call-update) | async-done | bytes 262160 | tf_op jit(solution)/shard_map/psum | solution.py:65
  500.7 2.7 gather_fusion
  503.6 0.7 copy.26
  504.6 11.7 %cholesky.164 = f32[128,128]{1,0:T(8,128)S(1)} custom-call(f32[128,128]{1,0:T(8,128)S(1)} %cholesky.197), custom_call_target="Cholesky" | custom-call | tf_op jit(solution)/shard_map/jit(cholesky)/cholesky | solution.py:12
  516.4 9.8 %custom-call.24 = f32[1,128,128]{1,2,0:T(8,128)S(1)} custom-call(f32[1,128,128]{2,1,0:T(8,128)S(1)} %get-tuple-element.291), custom_call_target="InvertDiagBlocksLowerTriangular" | custom-call | tf_op jit(solution)/shard_map/jit(cholesky)/cholesky | solution.py:12
  526.4 0.3 convolution_subtract_fusion.2
  526.7 11.7 %cholesky.181 = f32[128,128]{1,0:T(8,128)S(1)} custom-call(f32[128,128]{1,0:T(8,128)S(1)} %convolution_subtract_fusion.2), custom_call_target="Cholesky" | custom-call | tf_op jit(solution)/shard_map/jit(cholesky)/cholesky | solution.py:12
  538.4 0.7 compare_reduce_fusion.1
  539.1 0.6 compare_reduce_fusion
  539.8 28.4 %while.27 = (s32[]{:T(128)}, f32[256,256]{1,0:T(8,128)S(1)}, s32[]{:T(128)}, s32[4]{0:T(128)S(1)}, bf16[4,128,8192]{1,2,0:T(8,128)(2,1)}, /*index=5*/bf16[64,256...) while((s32[]{:T(128)}, f32[256,256]{1,0:T(8,128)S(1)}, ...), condition=%wide.region_12.14_spmd, body=%wide.region_10.13_spmd.sunk | while | flops 545292288 | bytes 11633126 | solution.py:80
  540.6 0.6 dynamic_slice.75
  543.1 1.7 constant_dynamic-slice_fusion.12
  544.8 3.5 copy.35
  549.1 4.6 multiply_reduce_fusion.6
  554.4 0.6 dynamic_slice.75
  556.9 1.7 constant_dynamic-slice_fusion.12
  558.6 3.5 copy.35
  562.9 4.6 multiply_reduce_fusion.6
  568.2 0.7 copy-done.2
  570.2 3.9 while.29
  570.2 0.6 fusion.65
  570.8 1.3 bitcast_dynamic-update-slice_fusion.5
  572.2 0.6 fusion.65
  572.8 1.3 bitcast_dynamic-update-slice_fusion.5
  574.1 19.7 %custom-call.19 = f32[2,128,128]{1,2,0:T(8,128)S(1)} custom-call(f32[2,128,128]{2,1,0:T(8,128)S(1)} %get-tuple-element.210), custom_call_target="InvertDiagBlocksLowerTriangular" | custom-call | tf_op jit(solution)/shard_map/triangular_solve | solution.py:13
  593.8 40.6 %reduce-scatter.2.cloned.1.call-done = f32[32,256]{1,0:T(8,128)} async-done(((f32[256,256]{1,0:T(8,128)}), f32[32,256]{1,0:T(8,128)}) %reduce-scatter.2.cloned.1.call-update) | async-done | bytes 32784 | tf_op jit(solution)/shard_map/reduce_scatter | solution.py:83
  634.4 0.9 fusion.18
  635.3 0.9 convolution_subtract_fusion.5
  637.0 78.5 %psum.31 = f32[256]{0:T(256)S(1)} all-reduce(f32[256]{0:T(256)S(1)} %multiply_reduce_fusion.2), channel_id=1, replica_groups=mesh['row'=8,'col'=32] {'row','col'}, use_global_device_ids=true, to_apply=%region_15.17 | all-reduce | flops 256 | bytes 2048 | tf_op jit(solution)/shard_map/psum | solution.py:85
  715.6 0.6 fusion.25
  (65 shorter events, 2.9 us)
Async XLA Ops:
  7.2 343.5 %all-reduce.7.cloned.1.call-start = ((), (), s32[]{:S(2)}) async-start(), calls=%async_computation.3 | async-start | bytes 1572864 | tf_op jit(solution)/shard_map/psum | solution.py:63
  10.5 12.0 %copy-start.3 = (f32[64,256]{1,0:T(8,128)S(1)}, f32[64,256]{1,0:T(8,128)}, u32[]{:S(2)}) copy-start(f32[64,256]{1,0:T(8,128)} %param.12) | copy-start | bytes 196612
  10.5 12.0 %copy-start.5 = (s32[4,1]{0,1:T(1,128)S(1)}, s32[4,1]{0,1:T(1,128)}, u32[]{:S(2)}) copy-start(s32[4,1]{0,1:T(1,128)} %param.13) | copy-start | bytes 52
  48.8 0.9 copy-start.1
  49.7 451.0 %all-reduce.5.cloned.1.call-start = ((), (), s32[]{:S(2)}) async-start(), calls=%async_computation.1 | async-start | bytes 524288 | tf_op jit(solution)/shard_map/psum | solution.py:65
  352.0 71.4 %copy-start.4 = (f32[512,256]{1,0:T(8,128)S(1)}, f32[512,256]{1,0:T(8,128)}, u32[]{:S(2)}) copy-start(f32[512,256]{1,0:T(8,128)} %get-tuple-element.280) | copy-start | bytes 1572868
  427.3 207.1 %reduce-scatter.2.cloned.1.call-start = ((), (), s32[]{:S(2)}) async-start(), calls=%async_computation.2 | async-start | bytes 294912 | tf_op jit(solution)/shard_map/reduce_scatter | solution.py:83
  500.7 3.6 copy-start
  568.2 0.7 copy-start.2
Sparse Core Ops, SparseCore 0:
  49.8 300.8 all-reduce.6
  427.4 73.2 all-reduce.4
  569.0 65.2 reduce-scatter.1
where the time goes:
time: 728 us; the launch traced here: 723 us
  waiting for transfers between devices  415 us (57%)
  other arithmetic  110 us (15%)
  blocking collectives  78.5 us (11%)
  local copies, waits for them, and re-layouts  48.6 us (7%)
  matrix products  28.2 us (4%)
  loops' own time  25.6 us (4%)
  between operations  16.9 us (2%)
    psum x1, waiting for transfers between devices, body(): sum_a = lax.psum(partial_a, 'col')  301 us
    psum x1, blocking collectives, body(): squares_b = lax.psum(jnp.sum(new_b * new_b, axis=0), ('row', 'col'))  78.5 us
    psum x1, waiting for transfers between devices, body(): gram_a = lax.psum(jnp.dot(new_full.T, new_full, precision=high), 'row')  73.3 us
    another operation x13, other arithmetic, solve_right(): lower = jnp.linalg.cholesky(matrix)  68.6 us
    reduce_scatter x1, waiting for transfers between devices, body(): part_b = lax.psum_scatter(partial_b, 'row', scatter_dimension=0, tiled=True)  40.6 us
    another operation x5, other arithmetic, solve_right(): lax.linalg.triangular_solve(lower, rows_in, left_side=False, lower=True,...  39.4 us
  transfers between devices with their start and end apart: 3, of which 3 were waited for; matrix products, arithmetic and copies ran while one was open for 3% of the time, Pallas kernels for 0%

commit v1 on v0

--- a/solution.py
+++ b/solution.py
@@ -6,6 +6,12 @@
 IB_DEV = 4
 JB_DEV = 2
 norm_eps = 1e-06
+
+
+def add_all(x, mesh_axis):
+    pieces = lax.all_gather(x, mesh_axis, axis=0, tiled=False)
+    acc = pieces.sum(axis=0)
+    return acc
 
 
 def solve_right(rows_in, matrix):
@@ -82,7 +88,7 @@
     )
     part_b = lax.psum_scatter(partial_b, "row", scatter_dimension=0, tiled=True)
     new_b = solve_right(part_b, v_two)
-    squares_b = lax.psum(jnp.sum(new_b * new_b, axis=0), ("row", "col"))
+    squares_b = add_all(jnp.sum(new_b * new_b, axis=0), ("row", "col"))
     scale_b = jnp.sqrt(squares_b / (col_slab * lax.axis_size("col")) + norm_eps)
     hat_b = new_b / scale_b[None, :]
     return (hat_a, hat_b)

time: 728 us -> 1000 us (1.37)
  blocking collectives: 78.5 us -> 350 us
    all_gather x0 -> x1, blocking collectives: none -> 350 us  [add_all(): pieces = lax.all_gather(x, mesh_axis, axis=0, tiled=False)]
    psum x1 -> x0, blocking collectives: 78.5 us -> none  [body(): squares_b = lax.psum(jnp.sum(new_b * new_b, axis=0), ('row', 'col'))]
  transfers between devices with their start and end apart: 3 -> 3, of which waited for: 3 -> 3; matrix products, arithmetic and copies ran while one was open for 3% -> 2% of each run, Pallas kernels for 0% -> 0%
where the time goes in v1:
time: 1000 us; the launch traced here: 995 us
  waiting for transfers between devices  415 us (42%)
  blocking collectives  350 us (35%)
  other arithmetic  110 us (11%)
  local copies, waits for them, and re-layouts  48.6 us (5%)
  matrix products  28.2 us (3%)
  loops' own time  25.6 us (3%)
  between operations  16.9 us (2%)
    all_gather x1, blocking collectives, add_all(): pieces = lax.all_gather(x, mesh_axis, axis=0, tiled=False)  350 us
    psum x1, waiting for transfers between devices, body(): sum_a = lax.psum(partial_a, 'col')  301 us
    psum x1, waiting for transfers between devices, body(): gram_a = lax.psum(jnp.dot(new_full.T, new_full, precision=high), 'row')  73.3 us
    another operation x13, other arithmetic, solve_right(): lower = jnp.linalg.cholesky(matrix)  68.6 us
    reduce_scatter x1, waiting for transfers between devices, body(): part_b = lax.psum_scatter(partial_b, 'row', scatter_dimension=0, tiled=True)  40.6 us
    another operation x5, other arithmetic, solve_right(): lax.linalg.triangular_solve(lower, rows_in, left_side=False, lower=True,...  39.4 us
  transfers between devices with their start and end apart: 3, of which 3 were waited for; matrix products, arithmetic and copies ran while one was open for 2% of the time, Pallas kernels for 0%

profile of v1, /device:TPU:1, one launch (start us, length us, event | category | flops | bytes accessed | tf_op | source)
XLA Modules:
  0.0 994.7 jit_solution(11345057057398367608)
XLA Ops:
  7.2 1.0 convert_element_type.22
  8.2 2.3 fusion.33
  10.5 12.0 %copy.29 = bf16[4,128,8192]{1,2,0:T(8,128)(2,1)} copy(bf16[4,128,8192]{2,1,0:T(8,128)(2,1)} %param.10) | data formatting | bytes 16777216 | tf_op jit(solution)/shard_map/while | solution.py:64
  22.5 26.2 %while.26 = (s32[]{:T(128)}, f32[512,256]{1,0:T(8,128)S(1)}, s32[]{:T(128)}, s32[4]{0:T(128)S(1)}, bf16[4,128,8192]{1,2,0:T(8,128)(2,1)}, /*index=5*/bf16[64,256...) while((s32[]{:T(128)}, f32[512,256]{1,0:T(8,128)S(1)}, ...), condition=%wide.region_2.3_spmd, body=%wide.region_0.2_spmd.sunk | while | flops 545292288 | bytes 11370982 | solution.py:64
  23.2 0.6 dynamic_slice.71
  26.1 1.7 constant_dynamic-slice_fusion.11
  27.8 3.5 copy.46
  31.3 4.0 multiply_reduce_fusion.5
  36.0 0.6 dynamic_slice.71
  38.9 1.7 constant_dynamic-slice_fusion.11
  40.6 3.5 copy.46
  44.1 4.0 multiply_reduce_fusion.5
  48.8 0.9 copy-done.1
  49.7 0.4 all-reduce.5.cloned.1.call-start
  50.1 300.5 %all-reduce.7.cloned.1.call-done = (f32[512,256]{1,0:T(8,128)}, f32[256,256]{0,1:T(8,128)}) async-done(((f32[512,256]{1,0:T(8,128)}, f32[256,256]{0,1:T(8,128)}), (f32[512,256]{1,0:T(8,128)}, f32[256,256]{0,1:T(8,128)})) %all-reduce.7.cloned.1.call-update) | async-done | bytes 786448 | tf_op jit(solution)/shard_map/psum | solution.py:69
  350.6 1.4 fusion.32
  352.2 11.7 %cholesky.130 = f32[128,128]{1,0:T(8,128)S(1)} custom-call(f32[128,128]{1,0:T(8,128)S(1)} %cholesky.194), custom_call_target="Cholesky" | custom-call | tf_op jit(solution)/shard_map/jit(cholesky)/cholesky | solution.py:18
  364.0 9.8 custom-call.23
  374.3 11.7 %cholesky.147 = f32[128,128]{1,0:T(8,128)S(1)} custom-call(f32[128,128]{1,0:T(8,128)S(1)} %convolution_subtract_fusion.3), custom_call_target="Cholesky" | custom-call | tf_op jit(solution)/shard_map/jit(cholesky)/cholesky | solution.py:18
  386.0 0.7 compare_reduce_fusion.2
  388.1 15.6 %while.28 = (s32[]{:T(128)}, f32[256,256]{1,0:T(8,128)S(1)}, s32[2,2]{1,0:T(2,128)S(1)}, f32[2,128,128]{2,1,0:T(8,128)S(1)}, s32[]{:T(128)}) while((s32[]{:T(128)}, f32[256,256]{1,0:T(8,128)S(1)}, s32[2,2]{1,0:T(2,128)S(1)}, f32[2,128,128]{2,1,0:T(8,128)S(1)}, s32[]{:T(128)}) %tuple.100), condition=%wide.while_cond, body=%wide.while_body.sunk | while | flops 2 | bytes 131189 | solution.py:19
  399.8 0.6 fusion.64
  400.4 1.4 bitcast_dynamic-update-slice_fusion.4
  401.8 0.6 fusion.64
  402.4 1.4 bitcast_dynamic-update-slice_fusion.4
  403.7 19.7 %custom-call.18 = f32[2,128,128]{1,2,0:T(8,128)S(1)} custom-call(f32[2,128,128]{2,1,0:T(8,128)S(1)} %get-tuple-element.202), custom_call_target="InvertDiagBlocksLowerTriangular" | custom-call | tf_op jit(solution)/shard_map/triangular_solve | solution.py:19
  423.4 0.4 fusion.4
  423.8 0.4 convolution_subtract_fusion.1
  424.2 0.4 fusion.16
  424.6 0.4 fusion.15
  425.0 0.6 convolution_subtract_fusion
  425.6 0.4 fusion.14
  425.9 1.3 fusion.3
  427.4 73.3 %all-reduce.5.cloned.1.call-done = f32[256,256]{0,1:T(8,128)} async-done(((f32[256,256]{0,1:T(8,128)}), f32[256,256]{0,1:T(8,128)}) %all-reduce.5.cloned.1.call-update) | async-done | bytes 262160 | tf_op jit(solution)/shard_map/psum | solution.py:71
  500.7 2.7 gather_fusion
  503.6 0.7 copy.38
  504.6 11.7 %cholesky.164 = f32[128,128]{1,0:T(8,128)S(1)} custom-call(f32[128,128]{1,0:T(8,128)S(1)} %cholesky.197), custom_call_target="Cholesky" | custom-call | tf_op jit(solution)/shard_map/jit(cholesky)/cholesky | solution.py:18
  516.4 9.8 custom-call.24
  526.4 0.3 convolution_subtract_fusion.2
  526.7 11.7 %cholesky.181 = f32[128,128]{1,0:T(8,128)S(1)} custom-call(f32[128,128]{1,0:T(8,128)S(1)} %convolution_subtract_fusion.2), custom_call_target="Cholesky" | custom-call | tf_op jit(solution)/shard_map/jit(cholesky)/cholesky | solution.py:18
  538.4 0.7 compare_reduce_fusion.1
  539.1 0.6 compare_reduce_fusion
  539.8 28.4 %while.27 = (s32[]{:T(128)}, f32[256,256]{1,0:T(8,128)S(1)}, s32[]{:T(128)}, s32[4]{0:T(128)S(1)}, bf16[4,128,8192]{1,2,0:T(8,128)(2,1)}, /*index=5*/bf16[64,256...) while((s32[]{:T(128)}, f32[256,256]{1,0:T(8,128)S(1)}, ...), condition=%wide.region_12.14_spmd, body=%wide.region_10.13_spmd.sunk | while | flops 545292288 | bytes 11633126 | solution.py:86
  540.6 0.6 dynamic_slice.75
  543.1 1.7 constant_dynamic-slice_fusion.12
  544.8 3.5 copy.47
  549.1 4.6 multiply_reduce_fusion.6
  554.4 0.6 dynamic_slice.75
  556.9 1.7 constant_dynamic-slice_fusion.12
  558.6 3.5 copy.47
  562.9 4.6 multiply_reduce_fusion.6
  568.2 0.7 copy-done.2
  570.2 3.9 while.29
  570.2 0.6 fusion.65
  570.8 1.3 bitcast_dynamic-update-slice_fusion.5
  572.2 0.6 fusion.65
  572.8 1.3 bitcast_dynamic-update-slice_fusion.5
  574.1 19.7 %custom-call.19 = f32[2,128,128]{1,2,0:T(8,128)S(1)} custom-call(f32[2,128,128]{2,1,0:T(8,128)S(1)} %get-tuple-element.210), custom_call_target="InvertDiagBlocksLowerTriangular" | custom-call | tf_op jit(solution)/shard_map/triangular_solve | solution.py:19
  593.8 40.6 %reduce-scatter.2.cloned.1.call-done = f32[32,256]{1,0:T(8,128)} async-done(((f32[256,256]{1,0:T(8,128)}), f32[32,256]{1,0:T(8,128)}) %reduce-scatter.2.cloned.1.call-update) | async-done | bytes 32784 | tf_op jit(solution)/shard_map/reduce_scatter | solution.py:89
  634.4 0.9 fusion.18
  635.3 0.9 convolution_subtract_fusion.5
  637.0 350.0 %all-gather.1 = f32[256,1,256]{2,1,0:T(1,128)S(1)} all-gather(f32[1,1,256]{2,1,0:T(1,128)S(1)} %bitcast.111), channel_id=2, replica_groups=mesh['row'=8,'col'=32] {'row','col'}, dimensions={0}, use_global_device_ids=true | all-gather | bytes 263168 | tf_op jit(solution)/shard_map/all_gather | solution.py:12
  987.0 0.3 reduce_sum.43
  987.3 0.6 fusion.25
  (66 shorter events, 3.2 us)
Async XLA Ops:
  7.2 343.5 %all-reduce.7.cloned.1.call-start = ((), (), s32[]{:S(2)}) async-start(), calls=%async_computation.3 | async-start | bytes 1572864 | tf_op jit(solution)/shard_map/psum | solution.py:69
  10.5 12.0 %copy-start.3 = (f32[64,256]{1,0:T(8,128)S(1)}, f32[64,256]{1,0:T(8,128)}, u32[]{:S(2)}) copy-start(f32[64,256]{1,0:T(8,128)} %param.12) | copy-start | bytes 196612
  10.5 12.0 %copy-start.5 = (s32[4,1]{0,1:T(1,128)S(1)}, s32[4,1]{0,1:T(1,128)}, u32[]{:S(2)}) copy-start(s32[4,1]{0,1:T(1,128)} %param.13) | copy-start | bytes 52
  48.8 0.9 copy-start.1
  49.7 451.0 %all-reduce.5.cloned.1.call-start = ((), (), s32[]{:S(2)}) async-start(), calls=%async_computation.1 | async-start | bytes 524288 | tf_op jit(solution)/shard_map/psum | solution.py:71
  352.0 71.4 %copy-start.4 = (f32[512,256]{1,0:T(8,128)S(1)}, f32[512,256]{1,0:T(8,128)}, u32[]{:S(2)}) copy-start(f32[512,256]{1,0:T(8,128)} %get-tuple-element.296) | copy-start | bytes 1572868
  427.3 207.1 %reduce-scatter.2.cloned.1.call-start = ((), (), s32[]{:S(2)}) async-start(), calls=%async_computation.2 | async-start | bytes 294912 | tf_op jit(solution)/shard_map/reduce_scatter | solution.py:89
  500.7 3.6 copy-start
  568.2 0.7 copy-start.2
Sparse Core Ops, SparseCore 0:
  49.8 300.8 all-reduce.6
  427.4 73.2 all-reduce.4
  569.0 65.2 reduce-scatter.1
